TPU v7x, 32 devices: a whole 2x2x4 slice. The times are simulated.
32 devices in a mesh: fish: 2 (over y), img: 16 (over z, x, core).
Axes of the slice: x: 2, y: 2, z: 4, core: 2. Of those that a mesh axis runs over, the one named last changes fastest.
Arguments:
- img_feat: bfloat16 [64, 16384], P(None, ('fish', 'img')), parts along dimension 1, may hold values from -80 to 80
- mdl_feat: bfloat16 [64, 2048], P(None, ('fish', 'img')), parts along dimension 1, may hold values from -80 to 80
- img_mass: float32 [16384], P(('fish', 'img')), parts along dimension 0, may hold values from 0.5 to 2
- mdl_mass: float32 [2048], P('fish'), parts along dimension 0, may hold values from 0.5 to 2
Outputs:
- grad_img: float32 [64, 16384], P(None, ('fish', 'img')), parts along dimension 1
- grad_mdl: float32 [64, 2048], P(None, ('fish', 'img')), parts along dimension 1
There are 2 independent parts, one for each index of `fish`. A program takes and returns all parts, laid end to end along the dimension named above; each array names one. Nothing has to cross between parts.
All inputs are finite; a program needn't handle non-finite values.
Results may differ from a plain program's by a relative error of at most 0.005.
Values may be sent and summed in bfloat16 or wider, within the bound.
No kernel may reach another device: no remote copies, remote signals or barrier semaphores. Data moves between devices by JAX's collectives and lax.ppermute only.
A program may use at most 64 MiB of HBM per device.

v0:
```python
import jax
import jax.numpy as jnp
from jax import lax
from jax.sharding import PartitionSpec as P

FEAT = 64
ITERS = 4
inv_temp = 20.0


def normalize(features):
    wide = features.astype(jnp.float32)
    guarded = jnp.mean(wide * wide, axis=0, keepdims=True) + 1e-06
    return (wide * lax.rsqrt(guarded)).astype(jnp.bfloat16)


def kernel_tile(imaged_unit, model_slice, factor):
    scores = lax.dot_general(
        imaged_unit, model_slice, (((0,), (0,)), ((), ())), preferred_element_type=jnp.float32
    )
    return jnp.exp(scores * factor).astype(jnp.bfloat16)


def shards(img_feat, mdl_feat, img_mass, mdl_mass):
    factor = inv_temp / FEAT
    imaged_unit = normalize(img_feat)
    model_unit = lax.all_gather(normalize(mdl_feat), "img", axis=1, tiled=True)
    total_model = model_unit.shape[1]
    share = mdl_feat.shape[1]
    local_rows = img_feat.shape[1]
    offset = lax.axis_index("img") * share
    kernel = kernel_tile(imaged_unit, model_unit, factor)
    col_scale = jnp.ones((total_model,), jnp.float32)
    col_low = col_scale.astype(jnp.bfloat16)
    row_scale = jnp.ones((local_rows,), jnp.float32)
    for iteration in range(ITERS):
        row_scale = img_mass / jnp.dot(kernel, col_low, preferred_element_type=jnp.float32)
        partial_cols = jnp.dot(
            row_scale.astype(jnp.bfloat16), kernel, preferred_element_type=jnp.float32
        )
        col_scale = mdl_mass / lax.psum(partial_cols, "img")
        col_low = col_scale.astype(jnp.bfloat16)
    weighted = (model_unit.astype(jnp.float32) * col_scale[None, :]).astype(jnp.bfloat16)
    grad_img = -(
        lax.dot_general(
            weighted, kernel, (((1,), (1,)), ((), ())), preferred_element_type=jnp.float32
        )
        * row_scale[None, :]
    )
    row_feat = (imaged_unit.astype(jnp.float32) * row_scale[None, :]).astype(jnp.bfloat16)
    summed = lax.psum_scatter(
        lax.dot_general(
            kernel, row_feat, (((0,), (1,)), ((), ())), preferred_element_type=jnp.float32
        ),
        "img",
        scatter_dimension=0,
        tiled=True,
    )
    own_scale = lax.dynamic_slice_in_dim(col_scale, offset, share, 0)
    grad_mdl = -(summed * own_scale[:, None]).T
    return (grad_img, grad_mdl)


def solution(mesh):
    placed = (P(None, ("fish", "img")), P(None, ("fish", "img")), P(("fish", "img")), P("fish"))
    return jax.shard_map(
        shards,
        mesh=mesh,
        in_specs=placed,
        out_specs=(P(None, ("fish", "img")), P(None, ("fish", "img"))),
        check_vma=False,
    )
```

profile of v0, /device:TPU:0, one launch (start us, length us, event | category | flops | bytes accessed | tf_op | source)
XLA Modules:
  0.0 188.4 jit_solution(11212692938415362139)
XLA Ops:
  7.2 0.0 reduce-scatter.2.cloned.1.call-start
  7.2 0.8 copy.7
  8.0 0.1 fusion.8
  8.1 0.1 fusion.9
  8.2 23.8 %all_gather.3 = bf16[64,1024]{0,1:T(8,128)(2,1)S(1)} all-gather(bf16[64,64]{0,1:T(8,128)(2,1)S(1)} %fusion.9), channel_id=1, replica_groups=mesh['fish'=2,'img'=16] {'img'}, dimensions={1}, use_global_device_ids=true | all-gather | bytes 139264 | tf_op jit(solution)/shard_map/all_gather | solution.py:27
  32.0 0.9 fusion.2
  32.9 0.0 copy-start.2
  32.9 1.3 exponential_convert_fusion
  34.2 0.0 copy-start.1
  34.2 0.4 fusion.10
  34.6 0.0 copy-done.2
  34.7 0.2 fusion.14
  34.9 29.8 %psum.28 = f32[1024]{0:T(1024)S(1)} all-reduce(f32[1024]{0:T(1024)S(1)} %bitcast.28), channel_id=1, replica_groups=mesh['fish'=2,'img'=16] {'img'}, use_global_device_ids=true, to_apply=%region_2.0 | all-reduce | flops 1024 | bytes 8192 | tf_op jit(solution)/shard_map/psum | solution.py:41
  64.7 0.0 copy-done.1
  64.7 0.4 fusion.15
  65.1 0.3 fusion.16
  65.4 29.5 %psum.29 = f32[1024]{0:T(1024)S(1)} all-reduce(f32[1024]{0:T(1024)S(1)} %bitcast.29), channel_id=1, replica_groups=mesh['fish'=2,'img'=16] {'img'}, use_global_device_ids=true, to_apply=%region_3.0 | all-reduce | flops 1024 | bytes 8192 | tf_op jit(solution)/shard_map/psum | solution.py:41
  94.9 0.4 fusion.17
  95.3 0.0 copy-start
  95.3 0.2 fusion.18
  95.5 29.5 %psum.30 = f32[1024]{0:T(1024)S(1)} all-reduce(f32[1024]{0:T(1024)S(1)} %bitcast.30), channel_id=1, replica_groups=mesh['fish'=2,'img'=16] {'img'}, use_global_device_ids=true, to_apply=%region_4.0 | all-reduce | flops 1024 | bytes 8192 | tf_op jit(solution)/shard_map/psum | solution.py:41
  125.0 0.4 fusion.19
  125.4 0.0 copy-done
  125.4 1.3 fusion.4
  126.7 0.0 reduce-scatter.2.cloned.1.call-update
  126.7 0.2 fusion.20
  127.0 29.5 %psum.31 = f32[1024]{0:T(1024)S(1)} all-reduce(f32[1024]{0:T(1024)S(1)} %bitcast.31), channel_id=1, replica_groups=mesh['fish'=2,'img'=16] {'img'}, use_global_device_ids=true, to_apply=%region_5.0 | all-reduce | flops 1024 | bytes 8192 | tf_op jit(solution)/shard_map/psum | solution.py:41
  156.5 0.1 dynamic_slice.3
  156.6 1.3 fusion
  157.9 22.0 %reduce-scatter.2.cloned.1.call-done = f32[64,64]{1,0:T(8,128)} async-done(((f32[1024,64]{1,0:T(8,128)}), f32[64,64]{1,0:T(8,128)}) %reduce-scatter.2.cloned.1.call-update) | async-done | bytes 16400 | tf_op jit(solution)/shard_map/reduce_scatter | solution.py:51
  180.0 0.8 negate_bitcast_fusion
  180.8 0.7 copy.8
  (17 shorter events, 0.1 us)
Async XLA Ops:
  7.2 172.8 %reduce-scatter.2.cloned.1.call-start = ((), (), s32[]{:S(2)}) async-start(), calls=%async_computation.1 | async-start | bytes 557056 | tf_op jit(solution)/shard_map/reduce_scatter | solution.py:51
  32.9 1.7 copy-start.2
  34.2 30.5 %copy-start.1 = (f32[1024]{0:T(1024)S(1)}, f32[1024]{0:T(1024)}, u32[]{:S(2)}) copy-start(f32[1024]{0:T(1024)} %param.7) | copy-start | bytes 12292
  95.3 30.1 %copy-start = (bf16[64,512]{1,0:T(8,128)(2,1)S(1)}, bf16[64,512]{1,0:T(8,128)(2,1)}, u32[]{:S(2)}) copy-start(bf16[64,512]{1,0:T(8,128)(2,1)} %param.4) | copy-start | bytes 196612
Sparse Core Ops, SparseCore 0:
  126.9 53.0 reduce-scatter.1
where the time goes:
time: 189 us; the launch traced here: 188 us
  blocking collectives  142 us (75%)
  waiting for transfers between devices  22.1 us (12%)
  between operations  14.1 us (7%)
  matrix products  6.44 us (3%)
  other arithmetic  1.98 us (1%)
    psum x4, blocking collectives, shards(): col_scale = mdl_mass / lax.psum(partial_cols, 'img')  118 us
    all_gather x1, blocking collectives, shards(): model_unit = lax.all_gather(normalize(mdl_feat), 'img', axis=1, tiled=True)  23.8 us
    reduce_scatter x1, waiting for transfers between devices, shards(): lax.psum_scatter(lax.dot_general(kernel, row_feat, (((0,), (1,)), ((), ()...  22 us
  transfers between devices with their start and end apart: 1, of which 1 were waited for; matrix products, arithmetic and copies ran while one was open for 1% of the time, Pallas kernels for 0%

commit v1 on v0

--- a/solution.py
+++ b/solution.py
@@ -38,7 +38,7 @@
         partial_cols = jnp.dot(
             row_scale.astype(jnp.bfloat16), kernel, preferred_element_type=jnp.float32
         )
-        col_scale = mdl_mass / lax.psum(partial_cols, "img")
+        col_scale = mdl_mass / jnp.sum(lax.all_gather(partial_cols, "img"), axis=0)
         col_low = col_scale.astype(jnp.bfloat16)
     weighted = (model_unit.astype(jnp.float32) * col_scale[None, :]).astype(jnp.bfloat16)
     grad_img = -(

time: 189 us -> 155 us (0.82)
  blocking collectives: 142 us -> 96.8 us
  waiting for transfers between devices: 22.1 us -> 33.7 us
    psum x4 -> x0, blocking collectives: 118 us -> none  [shards(): col_scale = mdl_mass / lax.psum(partial_cols, 'img')]
    all_gather x0 -> x4, blocking collectives: none -> 73 us  [shards(): col_scale = mdl_mass / jnp.sum(lax.all_gather(partial_cols, 'img'), axis=0)]
    reduce_scatter x1, waiting for transfers between devices: 22 us -> 33.7 us  [shards(): lax.psum_scatter(lax.dot_general(kernel, row_feat, (((0,), (1,)), ((), ()...]
where the time goes in v1:
time: 155 us
  blocking collectives  96.8 us (62%)
  waiting for transfers between devices  33.7 us (22%)
  between operations  14.2 us (9%)
  matrix products  6.42 us (4%)
  other arithmetic  2.03 us (1%)
  local copies, waits for them, and re-layouts  1.72 us (1%)
    all_gather x4, blocking collectives, shards(): col_scale = mdl_mass / jnp.sum(lax.all_gather(partial_cols, 'img'), axis=0)  73 us
    reduce_scatter x1, waiting for transfers between devices, shards(): lax.psum_scatter(lax.dot_general(kernel, row_feat, (((0,), (1,)), ((), ()...  33.7 us
    all_gather x1, blocking collectives, shards(): model_unit = lax.all_gather(normalize(mdl_feat), 'img', axis=1, tiled=True)  23.8 us
  transfers between devices with their start and end apart: 1, of which 1 were waited for; matrix products, arithmetic and copies ran while one was open for 1% of the time, Pallas kernels for 0%

profile of v1, /device:TPU:0, one launch (start us, length us, event | category | flops | bytes accessed | tf_op | source)
XLA Modules:
  0.0 154.9 jit_solution(436602811876738528)
XLA Ops:
  7.2 0.0 reduce-scatter.2.cloned.1.call-start
  7.2 0.8 copy.9
  8.0 0.1 fusion.8
  8.1 0.1 fusion.9
  8.2 23.8 %all_gather.27 = bf16[64,1024]{0,1:T(8,128)(2,1)S(1)} all-gather(bf16[64,64]{0,1:T(8,128)(2,1)S(1)} %fusion.9), channel_id=1, replica_groups=mesh['fish'=2,'img'=16] {'img'}, dimensions={1}, use_global_device_ids=true | all-gather | bytes 139264 | tf_op jit(solution)/shard_map/all_gather | solution.py:27
  32.0 0.9 fusion.2
  32.9 0.0 copy-start.2
  32.9 1.3 exponential_convert_fusion
  34.2 0.0 copy-start.1
  34.2 0.4 fusion.10
  34.6 0.0 copy-done.2
  34.7 0.2 fusion.14
  34.9 17.6 %all-gather = f32[16384]{0:T(1024)S(1)} all-gather(f32[1024]{0:T(1024)S(1)} %bitcast.29), channel_id=2, replica_groups=mesh['fish'=2,'img'=16] {'img'}, dimensions={0}, use_global_device_ids=true | all-gather | bytes 69632 | tf_op jit(solution)/shard_map/all_gather | solution.py:41
  52.5 0.0 copy-done.1
  52.6 0.4 fusion.15
  53.0 0.3 fusion.16
  53.2 18.9 %all-gather.1 = f32[16384]{0:T(1024)S(1)} all-gather(f32[1024]{0:T(1024)S(1)} %bitcast.30), channel_id=3, replica_groups=mesh['fish'=2,'img'=16] {'img'}, dimensions={0}, use_global_device_ids=true | all-gather | bytes 69632 | tf_op jit(solution)/shard_map/all_gather | solution.py:41
  72.2 0.4 fusion.17
  72.6 0.0 copy-start
  72.6 0.2 fusion.18
  72.9 17.6 %all-gather.2 = f32[16384]{0:T(1024)S(1)} all-gather(f32[1024]{0:T(1024)S(1)} %bitcast.31), channel_id=4, replica_groups=mesh['fish'=2,'img'=16] {'img'}, dimensions={0}, use_global_device_ids=true | all-gather | bytes 69632 | tf_op jit(solution)/shard_map/all_gather | solution.py:41
  90.6 0.4 fusion.19
  90.9 0.0 copy-done
  91.0 1.3 fusion.4
  92.2 0.0 reduce-scatter.2.cloned.1.call-update
  92.3 0.2 fusion.20
  92.5 18.9 %all-gather.3 = f32[16384]{0:T(1024)S(1)} all-gather(f32[1024]{0:T(1024)S(1)} %bitcast.28), channel_id=5, replica_groups=mesh['fish'=2,'img'=16] {'img'}, dimensions={0}, use_global_device_ids=true | all-gather | bytes 69632 | tf_op jit(solution)/shard_map/all_gather | solution.py:41
  111.5 0.1 dynamic_slice.3
  111.6 1.3 fusion
  112.9 33.7 %reduce-scatter.2.cloned.1.call-done = f32[64,64]{1,0:T(8,128)} async-done(((f32[1024,64]{1,0:T(8,128)}), f32[64,64]{1,0:T(8,128)}) %reduce-scatter.2.cloned.1.call-update) | async-done | bytes 16400 | tf_op jit(solution)/shard_map/reduce_scatter | solution.py:51
  146.6 0.8 negate_bitcast_fusion
  147.4 0.7 copy.10
  (25 shorter events, 0.3 us)
Async XLA Ops:
  7.2 139.4 %reduce-scatter.2.cloned.1.call-start = ((), (), s32[]{:S(2)}) async-start(), calls=%async_computation.1 | async-start | bytes 557056 | tf_op jit(solution)/shard_map/reduce_scatter | solution.py:51
  32.9 1.7 %copy-start.2 = (f32[512]{0:T(512)S(1)}, f32[512]{0:T(512)}, u32[]{:S(2)}) copy-start(f32[512]{0:T(512)} %param.6) | copy-start | bytes 6148
  34.2 18.3 %copy-start.1 = (f32[1024]{0:T(1024)S(1)}, f32[1024]{0:T(1024)}, u32[]{:S(2)}) copy-start(f32[1024]{0:T(1024)} %param.7) | copy-start | bytes 12292
  72.6 18.3 %copy-start = (bf16[64,512]{1,0:T(8,128)(2,1)S(1)}, bf16[64,512]{1,0:T(8,128)(2,1)}, u32[]{:S(2)}) copy-start(bf16[64,512]{1,0:T(8,128)(2,1)} %param.4) | copy-start | bytes 196612
Sparse Core Ops, SparseCore 0:
  92.4 54.1 reduce-scatter.1
